TPU v7x, 128 devices: a whole 4x4x4 slice. The times are simulated.
128 devices in a mesh: dp: 2 (over core), expert: 64 (over y, x, z).
Axes of the slice: x: 4, y: 4, z: 4, core: 2. Of those that a mesh axis runs over, the one named last changes fastest.
Arguments:
- tokens: bfloat16 [16384, 2048], P(('dp', 'expert')), may hold values from -6 to 6
- cotangent: bfloat16 [16384, 2048], P(('dp', 'expert')), may hold values from -6 to 6
- routes: int32 [16384, 2], P(('dp', 'expert')), may hold values from 0 to 15, all different within a row; in each aligned block of 128 rows (0 to 127, 128 to 255, ...) at most 24 rows name the same one
- gates: float32 [16384, 2], P(('dp', 'expert')), may hold values from 0.1 to 1
- capacity: int32 [16], replicated, may hold values from 13 to 24, as said below
- layout: int32 [64], replicated, may hold values from 0 to 63, each once
- partner: int32 [64], replicated, may hold values from 0 to 63, as said below
- w_in: float32 [64, 2048, 256], P('expert'), may hold values from -0.125 to 0.125
- w_out: float32 [64, 256, 2048], P('expert'), may hold values from -0.1875 to 0.1875
- m_in: bfloat16 [64, 2048, 256], P('expert'), may hold values from -5 to 5
- v_in: bfloat16 [64, 2048, 256], P('expert'), may hold values from 0.099609375 to 4
- m_out: bfloat16 [64, 256, 2048], P('expert'), may hold values from -5 to 5
- v_out: bfloat16 [64, 256, 2048], P('expert'), may hold values from 0.099609375 to 4
Outputs:
- mixed: bfloat16 [16384, 2048], P(('dp', 'expert'))
- token_grad: bfloat16 [16384, 2048], P(('dp', 'expert'))
- new_w_in: float32 [64, 2048, 256], P('expert')
- new_w_out: float32 [64, 256, 2048], P('expert')
- new_m_in: bfloat16 [64, 2048, 256], P('expert')
- new_v_in: bfloat16 [64, 2048, 256], P('expert')
- new_m_out: bfloat16 [64, 256, 2048], P('expert')
- new_v_out: bfloat16 [64, 256, 2048], P('expert')
Inputs may be any that keep to these rules, and one draw needn't show every extreme that they name: `routes`: in the rows of one device no expert is named by more than 24 pairs, a bound that some block reaches; each token names 2 different experts. `capacity`: some expert has exactly 24 and some other exactly that minimum. `layout`: A permutation. partner[d] is d or the index half the expert axis away, and partner[partner[d]] = d; both kinds occur.
All inputs are finite; a program needn't handle non-finite values.
Results may differ from a plain program's by a relative error of at most 0.0079.
Values may be sent and summed in bfloat16 or wider, within the bound.
A program may use at most 128 MiB of HBM per device.

v0:
```python
import jax
import jax.numpy as jnp
from jax import lax
from jax.sharding import PartitionSpec as P

GROUP = 4


def relay(block, step):
    ndp = lax.axis_size("dp")
    nexp = lax.axis_size("expert")
    route = []
    for d in range(ndp):
        sign = 1 if d % 2 == 0 else -1
        for e in range(nexp):
            route.append((d * nexp + e, d * nexp + (e + sign * step) % nexp))
    return lax.ppermute(block, ("dp", "expert"), route)


def migrate(blocks):
    ndp = lax.axis_size("dp")
    step = lax.axis_size("expert") // 4
    here = lax.axis_index("dp")
    halves = tuple(
        (
            lax.dynamic_slice_in_dim(b, here * (b.shape[0] // ndp), b.shape[0] // ndp, 0)
            for b in blocks
        )
    )
    moved = relay(relay(halves, step), step)
    return tuple((lax.all_gather(m, "dp", axis=0, tiled=True) for m in moved))


def gelu_tanh(value):
    return jax.nn.gelu(value, approximate=True)


def adamw(weight, first, second, grad):
    first_f = 0.9 * first.astype(jnp.float32) + 0.1 * grad
    second_f = 0.999 * second.astype(jnp.float32) + 0.001 * grad * grad
    corrected = first_f / (1.0 - 0.9**10) / (jnp.sqrt(second_f / (1.0 - 0.999**10)) + 1e-08)
    updated = weight - 0.01 * (corrected + 0.1 * weight)
    return (updated, first_f.astype(jnp.bfloat16), second_f.astype(jnp.bfloat16))


def local(
    tokens,
    cotangent,
    routes,
    gates,
    capacity,
    layout,
    partner,
    w_in,
    w_out,
    m_in,
    v_in,
    m_out,
    v_out,
):
    width = tokens.shape[1]
    count = tokens.shape[0]
    topk = routes.shape[1]
    experts = capacity.shape[0]
    slots = 3 * count * topk // (2 * experts)
    nexp = lax.axis_size("expert")
    here = lax.axis_index("expert")
    moved = jnp.take(partner, here) != here
    flat_routes = routes.reshape(-1)
    onehot = (flat_routes[:, None] == jnp.arange(experts, dtype=jnp.int32)[None, :]).astype(
        jnp.int32
    )
    position = jnp.sum((jnp.cumsum(onehot, 0) - 1) * onehot, 1)
    limit = jnp.sum(onehot * capacity[None, :], 1)
    slot = jnp.where(position < limit, flat_routes * slots + position, experts * slots)
    x_rows = jnp.repeat(tokens, topk, axis=0)
    scaled = (
        gates.reshape(-1)[:, None] * jnp.repeat(cotangent, topk, axis=0).astype(jnp.float32)
    ).astype(jnp.bfloat16)

    def build(rows):
        filled = jnp.zeros((experts * slots + 1, width), jnp.bfloat16).at[slot].set(rows)
        return filled[:-1].reshape(experts, slots, width)

    x_buf = build(x_rows)
    g_buf = build(scaled)
    weight_in, weight_out = (w_in[0], w_out[0])
    first_in, second_in, first_out, second_out = (m_in[0], v_in[0], m_out[0], v_out[0])
    held = jnp.take(layout, partner, axis=0)
    other = migrate(
        (
            weight_in.astype(jnp.bfloat16),
            weight_out.astype(jnp.bfloat16),
            first_in,
            second_in,
            first_out,
            second_out,
        )
    )
    other_w = (other[0].astype(weight_in.dtype), other[1].astype(weight_out.dtype))
    other_m = other[2:]
    weight_in = jnp.where(moved, other_w[0], weight_in)
    weight_out = jnp.where(moved, other_w[1], weight_out)
    first_in = jnp.where(moved, other_m[0], first_in)
    second_in = jnp.where(moved, other_m[1], second_in)
    first_out = jnp.where(moved, other_m[2], first_out)
    second_out = jnp.where(moved, other_m[3], second_out)
    target_expert = held // GROUP
    send_x = jnp.take(x_buf, target_expert, axis=0)
    send_g = jnp.take(g_buf, target_expert, axis=0)
    recv_x, recv_g = (
        lax.all_to_all(send_x, "expert", split_axis=0, concat_axis=0, tiled=True),
        lax.all_to_all(send_g, "expert", split_axis=0, concat_axis=0, tiled=True),
    )
    rows = recv_x.reshape(-1, width)
    grows = recv_g.reshape(-1, width)
    wb_in = weight_in.astype(jnp.bfloat16)
    wb_out = weight_out.astype(jnp.bfloat16)
    pre = jnp.dot(rows, wb_in, preferred_element_type=jnp.float32)
    hidden, pull = jax.vjp(gelu_tanh, pre)
    hidden = hidden.astype(jnp.bfloat16)
    part = jnp.dot(hidden, wb_out, preferred_element_type=jnp.float32).astype(jnp.bfloat16)
    dhid = lax.dot_general(
        grows, wb_out, (((1,), (1,)), ((), ())), preferred_element_type=jnp.float32
    )
    dpre = pull(dhid)[0].astype(jnp.bfloat16)
    xpart = lax.dot_general(
        dpre, wb_in, (((1,), (1,)), ((), ())), preferred_element_type=jnp.float32
    ).astype(jnp.bfloat16)
    grad_in = lax.dot_general(
        rows, dpre, (((0,), (0,)), ((), ())), preferred_element_type=jnp.float32
    )
    grad_out = lax.dot_general(
        hidden, grows, (((0,), (0,)), ((), ())), preferred_element_type=jnp.float32
    )
    back_part, back_dx = (
        lax.all_to_all(
            part.reshape(nexp, slots, width), "expert", split_axis=0, concat_axis=0, tiled=True
        ),
        lax.all_to_all(
            xpart.reshape(nexp, slots, width), "expert", split_axis=0, concat_axis=0, tiled=True
        ),
    )
    grad_in, grad_out = lax.psum((grad_in, grad_out), "dp")
    new_w_in, new_m_in, new_v_in = adamw(weight_in, first_in, second_in, grad_in)
    new_w_out, new_m_out, new_v_out = adamw(weight_out, first_out, second_out, grad_out)
    owners = (target_expert[:, None] == jnp.arange(experts, dtype=jnp.int32)[None, :]).astype(
        jnp.bfloat16
    )
    out_sum = jnp.einsum("je,jcd->ecd", owners, back_part, preferred_element_type=jnp.float32)
    dx_sum = jnp.einsum("je,jcd->ecd", owners, back_dx, preferred_element_type=jnp.float32)
    blank = jnp.zeros((1, width), jnp.float32)
    out_vals = jnp.take(jnp.concatenate([out_sum.reshape(-1, width), blank]), slot, axis=0)
    dx_vals = jnp.take(jnp.concatenate([dx_sum.reshape(-1, width), blank]), slot, axis=0)
    mixed = jnp.sum(out_vals.reshape(count, topk, width) * gates[:, :, None], axis=1).astype(
        jnp.bfloat16
    )
    token_grad = jnp.sum(dx_vals.reshape(count, topk, width), axis=1).astype(jnp.bfloat16)
    return (
        mixed,
        token_grad,
        new_w_in[None],
        new_w_out[None],
        new_m_in[None],
        new_v_in[None],
        new_m_out[None],
        new_v_out[None],
    )


def solution(mesh):
    in_specs = (
        P(("dp", "expert"), None),
        P(("dp", "expert"), None),
        P(("dp", "expert"), None),
        P(("dp", "expert"), None),
        P(),
        P(),
        P(),
        P("expert", None, None),
        P("expert", None, None),
        P("expert", None, None),
        P("expert", None, None),
        P("expert", None, None),
        P("expert", None, None),
    )
    out_specs = (
        P(("dp", "expert"), None),
        P(("dp", "expert"), None),
        P("expert", None, None),
        P("expert", None, None),
        P("expert", None, None),
        P("expert", None, None),
        P("expert", None, None),
        P("expert", None, None),
    )
    return jax.shard_map(local, mesh=mesh, in_specs=in_specs, out_specs=out_specs, check_vma=False)
```

profile of v0, /device:TPU:1, one launch (start us, length us, event | category | flops | bytes accessed | tf_op | source)
XLA Modules:
  0.0 611.7 jit_solution(7909800098683608369)
XLA Ops:
  35.7 8.4 %broadcast_select_fusion = (bf16[64,24,2048]{2,1,0:T(8,128)(2,1)}, bf16[64,24,2048]{2,1,0:T(8,128)(2,1)S(1)}) fusion(bf16[64,24,2048]{2,1,0:T(8,128)(2,1)} %gather_fusion.3, pred[64]{0:T(512)(128)(4,1)S(1)} %get-tuple-element.27, bf16[64,24,2048]{2,1,0:T(8,128)(2,1)} %gather_fusion.1), kind=kLoop, calls=%fused_computation.13 | loop fusion | flops 6291456 | bytes 25165888 | tf_op jit(solution)/shard_map/jit(_take)/select_n | solution.py:110
  44.1 84.6 %all_to_all.20 = bf16[64,24,2048]{2,1,0:T(8,128)(2,1)} all-to-all(bf16[64,24,2048]{2,1,0:T(8,128)(2,1)S(1)} %get-tuple-element.38), channel_id=1, replica_groups=mesh['dp'=2,'expert'=64] {'expert'}, dimensions={0} | all-to-all | bytes 12582912 | tf_op jit(solution)/shard_map/all_to_all | solution.py:112
  128.6 6.5 %all-to-all-start.2 = ((bf16[64,24,2048]{2,1,0:T(8,128)(2,1)}), bf16[64,24,2048]{2,1,0:T(8,128)(2,1)}, u32[]{:S(2)}, u32[]{:S(2)}) async-start(bf16[64,24,2048]{2,1,0:T(8,128)(2,1)} %get-tuple-element.37), calls=%async_computation.2 | async-start | bytes 12582912 | tf_op jit(solution)/shard_map/all_to_all | solution.py:113
  138.9 74.9 %collective-permute-done = bf16[1024,256]{1,0:T(8,128)(2,1)} collective-permute-done((bf16[1024,256]{1,0:T(8,128)(2,1)S(1)}, bf16[1024,256]{1,0:T(8,128)(2,1)}, u32[]{:S(2)}, u32[]{:S(2)}) %collective-permute-start) | collective-permute-done | bytes 524320 | tf_op jit(solution)/shard_map/ppermute | solution.py:17
  215.4 7.1 %collective-permute-done.1 = bf16[1024,256]{1,0:T(8,128)(2,1)S(1)} collective-permute-done((bf16[1024,256]{1,0:T(8,128)(2,1)}, bf16[1024,256]{1,0:T(8,128)(2,1)S(1)}, u32[]{:S(2)}, u32[]{:S(2)}) %collective-permute-start.1) | collective-permute-done | bytes 524320 | tf_op jit(solution)/shard_map/ppermute | solution.py:17
  229.2 7.6 %collective-permute-done.3 = bf16[128,2048]{1,0:T(8,128)(2,1)S(1)} collective-permute-done((bf16[128,2048]{1,0:T(8,128)(2,1)}, bf16[128,2048]{1,0:T(8,128)(2,1)S(1)}, u32[]{:S(2)}, u32[]{:S(2)}) %collective-permute-start.3) | collective-permute-done | bytes 524320 | tf_op jit(solution)/shard_map/ppermute | solution.py:17
  245.1 12.8 %all-gather.9.cloned.1.call-done = bf16[256,2048]{1,0:T(8,128)(2,1)} async-done(((bf16[128,2048]{1,0:T(8,128)(2,1)}), bf16[256,2048]{1,0:T(8,128)(2,1)}) %all-gather.9.cloned.1.call-update) | async-done | bytes 1048592 | tf_op jit(solution)/shard_map/all_gather | solution.py:31
  259.5 5.7 fusion.37
  265.3 6.0 fusion.12
  275.8 10.3 %all-to-all-start.3 = ((bf16[64,24,2048]{2,1,0:T(8,128)(2,1)}), bf16[64,24,2048]{2,1,0:T(8,128)(2,1)}, u32[]{:S(2)}, u32[]{:S(2)}) async-start(bf16[64,24,2048]{2,1,0:T(8,128)(2,1)} %bitcast.95), calls=%async_computation.3 | async-start | bytes 12582912 | tf_op jit(solution)/shard_map/all_to_all | solution.py:140
  289.7 75.4 %collective-permute-done.8 = bf16[128,2048]{1,0:T(8,128)(2,1)S(1)} collective-permute-done((bf16[128,2048]{1,0:T(8,128)(2,1)S(1)}, bf16[128,2048]{1,0:T(8,128)(2,1)S(1)}, u32[]{:S(2)}, u32[]{:S(2)}) %collective-permute-start.8) | collective-permute-done | bytes 524320 | tf_op jit(solution)/shard_map/ppermute | solution.py:17
  373.6 5.5 collective-permute-done.10
  381.5 6.4 %collective-permute-done.11 = bf16[128,2048]{1,0:T(8,128)(2,1)} collective-permute-done((bf16[128,2048]{1,0:T(8,128)(2,1)}, bf16[128,2048]{1,0:T(8,128)(2,1)}, u32[]{:S(2)}, u32[]{:S(2)}) %collective-permute-start.11) | collective-permute-done | bytes 524320 | tf_op jit(solution)/shard_map/ppermute | solution.py:17
  388.4 7.0 %fusion.36 = f32[256,2048]{1,0:T(8,128)} fusion(bf16[1536,2048]{1,0:T(8,128)(2,1)} %bitcast.14, f32[1536,256]{1,0:T(8,128)} %fusion.37), kind=kOutput, calls=%fused_computation.94 | convolution fusion | flops 1614151680 | bytes 9961472 | tf_op jit(solution)/shard_map/dot_general | solution.py:133
  395.4 6.0 fusion.38
  401.5 6.0 convolution_convert_fusion.1
  407.5 15.6 %all-to-all-start.1 = ((bf16[64,24,2048]{2,1,0:T(8,128)(2,1)}), bf16[64,24,2048]{2,1,0:T(8,128)(2,1)}, u32[]{:S(2)}, u32[]{:S(2)}) async-start(bf16[64,24,2048]{2,1,0:T(8,128)(2,1)} %bitcast.94), calls=%async_computation.1 | async-start | bytes 12582912 | tf_op jit(solution)/shard_map/all_to_all | solution.py:137
  425.6 74.8 %collective-permute-done.4 = bf16[1024,256]{1,0:T(8,128)(2,1)S(1)} collective-permute-done((bf16[1024,256]{1,0:T(8,128)(2,1)S(1)}, bf16[1024,256]{1,0:T(8,128)(2,1)S(1)}, u32[]{:S(2)}, u32[]{:S(2)}) %collective-permute-start.4) | collective-permute-done | bytes 524320 | tf_op jit(solution)/shard_map/ppermute | solution.py:17
  515.8 7.0 %collective-permute-done.7 = bf16[1024,256]{1,0:T(8,128)(2,1)S(1)} collective-permute-done((bf16[1024,256]{1,0:T(8,128)(2,1)}, bf16[1024,256]{1,0:T(8,128)(2,1)S(1)}, u32[]{:S(2)}, u32[]{:S(2)}) %collective-permute-start.7) | collective-permute-done | bytes 524320 | tf_op jit(solution)/shard_map/ppermute | solution.py:17
  523.8 7.8 %fusion.20 = (bf16[1,256,2048]{2,1,0:T(8,128)(2,1)}, f32[1,256,2048]{2,1,0:T(8,128)}, bf16[1,256,2048]{2,1,0:T(8,128)(2,1)}) fusion(f32[256,2048]{1,0:T(8,128)} %get-tuple-element.24, bf16[256,2048]{1,0:T(8,128)(2,1)} %all-gather.17.cloned.1.call-done, bf16[1,256,2048]{2,1,0:T(8,128)(2,1)} %param.29, pred[]{:T(512)S(6)} %ne.24, ...), kind=kLoop, calls=%fused_computation.44 | loop fusion | flops 12058624 | bytes 13631489 | tf_op jit(solution)/shard_map/broadcast_in_dim | solution.py:167
  531.6 13.2 %all-gather.13.cloned.1.call-done = bf16[2048,256]{1,0:T(8,128)(2,1)} async-done(((bf16[1024,256]{1,0:T(8,128)(2,1)}), bf16[2048,256]{1,0:T(8,128)(2,1)}) %all-gather.13.cloned.1.call-update) | async-done | bytes 1048592 | tf_op jit(solution)/shard_map/all_gather | solution.py:31
  544.8 8.1 %fusion.19 = (bf16[1,2048,256]{2,1,0:T(8,128)(2,1)}, f32[1,2048,256]{2,1,0:T(8,128)}, bf16[1,2048,256]{2,1,0:T(8,128)(2,1)}) fusion(f32[2048,256]{1,0:T(8,128)} %get-tuple-element.23, bf16[2048,256]{1,0:T(8,128)(2,1)} %all-gather.13.cloned.1.call-done, bf16[1,2048,256]{2,1,0:T(8,128)(2,1)} %param.27, pred[]{:T(512)S(6)} %ne.24, ...), kind=kLoop, calls=%fused_computation.43 | loop fusion | flops 12058624 | bytes 13631489 | tf_op jit(solution)/shard_map/broadcast_in_dim | solution.py:165
  552.9 9.7 %fusion = f32[16,24,2048]{2,0,1:T(8,128)S(1)} fusion(bf16[64,24,2048]{2,1,0:T(8,128)(2,1)} %all-to-all-done.3, s32[64]{0:T(128)S(1)} %get-tuple-element.28), kind=kOutput, calls=%fused_computation.9 | convolution fusion | flops 100664320 | bytes 9437440 | tf_op jit(solution)/shard_map/je,jcd->ecd/dot_general | solution.py:151
  564.4 9.5 %fusion.2 = f32[16,24,2048]{2,0,1:T(8,128)S(1)} fusion(bf16[64,24,2048]{2,1,0:T(8,128)(2,1)} %all-to-all-done.1, s32[64]{0:T(128)S(1)} %get-tuple-element.28), kind=kOutput, calls=%fused_computation.11 | convolution fusion | flops 100664320 | bytes 9437440 | tf_op jit(solution)/shard_map/je,jcd->ecd/dot_general | solution.py:150
  (127 shorter events, 120.2 us)
Async XLA Ops:
  128.6 85.4 %copy-start.3 = (f32[1,256,2048]{2,1,0:T(8,128)S(1)}, f32[1,256,2048]{2,1,0:T(8,128)}, u32[]{:S(2)}) copy-start(f32[1,256,2048]{2,1,0:T(8,128)} %param.25) | copy-start | bytes 6291460
  128.6 136.7 %all-to-all-start.2 = ((bf16[64,24,2048]{2,1,0:T(8,128)(2,1)}), bf16[64,24,2048]{2,1,0:T(8,128)(2,1)}, u32[]{:S(2)}, u32[]{:S(2)}) async-start(bf16[64,24,2048]{2,1,0:T(8,128)(2,1)} %get-tuple-element.37), calls=%async_computation.2 | async-start | bytes 12582912 | tf_op jit(solution)/shard_map/all_to_all | solution.py:113
  135.1 106.9 %all-gather.7.cloned.1.call-start = ((), (), s32[]{:S(2)}) async-start(), calls=%async_computation.4 | async-start | bytes 1572864 | tf_op jit(solution)/shard_map/all_gather | solution.py:31
  136.4 77.4 %collective-permute-start = (bf16[1024,256]{1,0:T(8,128)(2,1)S(1)}, bf16[1024,256]{1,0:T(8,128)(2,1)}, u32[]{:S(2)}, u32[]{:S(2)}) collective-permute-start(bf16[1024,256]{1,0:T(8,128)(2,1)S(1)} %dynamic-slice_convert_fusion.1), channel_id=1, source_target_pairs={{0,16},{1,17},{2,18},{3,19},{4,20},{5,21},{6,22},{7,23},{8,24},{9,... | collective-permute-start | bytes 1572872 | tf_op jit(solution)/shard_map/ppermute | solution.py:17
  213.8 8.7 %collective-permute-start.1 = (bf16[1024,256]{1,0:T(8,128)(2,1)}, bf16[1024,256]{1,0:T(8,128)(2,1)S(1)}, u32[]{:S(2)}, u32[]{:S(2)}) collective-permute-start(bf16[1024,256]{1,0:T(8,128)(2,1)} %collective-permute-done), channel_id=1, source_target_pairs={{0,16},{1,17},{2,18},{3,19},{4,20},{5,21},{6,22},{7,23},{8,24},{9,... | collective-permute-start | bytes 1572872 | tf_op jit(solution)/shard_map/ppermute | solution.py:17
  214.1 14.2 %collective-permute-start.2 = (bf16[128,2048]{1,0:T(8,128)(2,1)S(1)}, bf16[128,2048]{1,0:T(8,128)(2,1)}, u32[]{:S(2)}, u32[]{:S(2)}) collective-permute-start(bf16[128,2048]{1,0:T(8,128)(2,1)S(1)} %dynamic-slice_convert_fusion), channel_id=1, source_target_pairs={{0,16},{1,17},{2,18},{3,19},{4,20},{5,21},{6,22},{7,23},{8,24},{9,... | collective-permute-start | bytes 1572872 | tf_op jit(solution)/shard_map/ppermute | solution.py:17
  223.3 34.5 %all-gather.9.cloned.1.call-start = ((), (), s32[]{:S(2)}) async-start(), calls=%async_computation.5 | async-start | bytes 1572864 | tf_op jit(solution)/shard_map/all_gather | solution.py:31
  228.3 8.5 %collective-permute-start.3 = (bf16[128,2048]{1,0:T(8,128)(2,1)}, bf16[128,2048]{1,0:T(8,128)(2,1)S(1)}, u32[]{:S(2)}, u32[]{:S(2)}) collective-permute-start(bf16[128,2048]{1,0:T(8,128)(2,1)} %collective-permute-done.2), channel_id=1, source_target_pairs={{0,16},{1,17},{2,18},{3,19},{4,20},{5,21},{6,22},{7,23},{8,24},{9,... | collective-permute-start | bytes 1572872 | tf_op jit(solution)/shard_map/ppermute | solution.py:17
  275.8 131.7 %all-to-all-start.3 = ((bf16[64,24,2048]{2,1,0:T(8,128)(2,1)}), bf16[64,24,2048]{2,1,0:T(8,128)(2,1)}, u32[]{:S(2)}, u32[]{:S(2)}) async-start(bf16[64,24,2048]{2,1,0:T(8,128)(2,1)} %bitcast.95), calls=%async_computation.3 | async-start | bytes 12582912 | tf_op jit(solution)/shard_map/all_to_all | solution.py:140
  286.1 237.6 %all-gather.15.cloned.1.call-start = ((), (), s32[]{:S(2)}) async-start(), calls=%async_computation.8 | async-start | bytes 1572864 | tf_op jit(solution)/shard_map/all_gather | solution.py:31
  287.3 77.8 %collective-permute-start.8 = (bf16[128,2048]{1,0:T(8,128)(2,1)S(1)}, bf16[128,2048]{1,0:T(8,128)(2,1)S(1)}, u32[]{:S(2)}, u32[]{:S(2)}) collective-permute-start(bf16[128,2048]{1,0:T(8,128)(2,1)S(1)} %dynamic-slice_bitcast_fusion.1), channel_id=1, source_target_pairs={{0,16},{1,17},{2,18},{3,19},{4,20},{5,21},{6,22},{7,23},{8,24},{9,... | collective-permute-start | bytes 1572872 | tf_op jit(solution)/shard_map/ppermute | solution.py:17
  365.1 8.4 %collective-permute-start.9 = (bf16[128,2048]{1,0:T(8,128)(2,1)S(1)}, bf16[128,2048]{1,0:T(8,128)(2,1)}, u32[]{:S(2)}, u32[]{:S(2)}) collective-permute-start(bf16[128,2048]{1,0:T(8,128)(2,1)S(1)} %collective-permute-done.8), channel_id=1, source_target_pairs={{0,16},{1,17},{2,18},{3,19},{4,20},{5,21},{6,22},{7,23},{8,24},{9,... | collective-permute-start | bytes 1572872 | tf_op jit(solution)/shard_map/ppermute | solution.py:17
  368.4 10.7 %collective-permute-start.10 = (bf16[128,2048]{1,0:T(8,128)(2,1)}, bf16[128,2048]{1,0:T(8,128)(2,1)}, u32[]{:S(2)}, u32[]{:S(2)}) collective-permute-start(bf16[128,2048]{1,0:T(8,128)(2,1)} %dynamic-slice_bitcast_fusion), channel_id=1, source_target_pairs={{0,16},{1,17},{2,18},{3,19},{4,20},{5,21},{6,22},{7,23},{8,24},{9,... | collective-permute-start | bytes 1572872 | tf_op jit(solution)/shard_map/ppermute | solution.py:17
  373.5 150.2 %all-gather.17.cloned.1.call-start = ((), (), s32[]{:S(2)}) async-start(), calls=%async_computation.9 | async-start | bytes 1572864 | tf_op jit(solution)/shard_map/all_gather | solution.py:31
  379.1 8.8 %collective-permute-start.11 = (bf16[128,2048]{1,0:T(8,128)(2,1)}, bf16[128,2048]{1,0:T(8,128)(2,1)}, u32[]{:S(2)}, u32[]{:S(2)}) collective-permute-start(bf16[128,2048]{1,0:T(8,128)(2,1)} %collective-permute-done.10), channel_id=1, source_target_pairs={{0,16},{1,17},{2,18},{3,19},{4,20},{5,21},{6,22},{7,23},{8,24},{9,... | collective-permute-start | bytes 1572872 | tf_op jit(solution)/shard_map/ppermute | solution.py:17
  388.0 135.8 %all-reduce.5.cloned.1.call-start = ((), (), s32[]{:S(2)}) async-start(), calls=%async_computation.10 | async-start | bytes 8388608 | tf_op jit(solution)/shard_map/psum | solution.py:144
  407.5 157.0 %all-to-all-start.1 = ((bf16[64,24,2048]{2,1,0:T(8,128)(2,1)}), bf16[64,24,2048]{2,1,0:T(8,128)(2,1)}, u32[]{:S(2)}, u32[]{:S(2)}) async-start(bf16[64,24,2048]{2,1,0:T(8,128)(2,1)} %bitcast.94), calls=%async_computation.1 | async-start | bytes 12582912 | tf_op jit(solution)/shard_map/all_to_all | solution.py:137
  423.1 108.5 %all-gather.11.cloned.1.call-start = ((), (), s32[]{:S(2)}) async-start(), calls=%async_computation.6 | async-start | bytes 1572864 | tf_op jit(solution)/shard_map/all_gather | solution.py:31
  423.2 77.2 %collective-permute-start.4 = (bf16[1024,256]{1,0:T(8,128)(2,1)S(1)}, bf16[1024,256]{1,0:T(8,128)(2,1)S(1)}, u32[]{:S(2)}, u32[]{:S(2)}) collective-permute-start(bf16[1024,256]{1,0:T(8,128)(2,1)S(1)} %dynamic-slice_bitcast_fusion.3), channel_id=1, source_target_pairs={{0,16},{1,17},{2,18},{3,19},{4,20},{5,21},{6,22},{7,23},{8,24},{9,... | collective-permute-start | bytes 1572872 | tf_op jit(solution)/shard_map/ppermute | solution.py:17
  500.4 8.3 %collective-permute-start.5 = (bf16[1024,256]{1,0:T(8,128)(2,1)S(1)}, bf16[1024,256]{1,0:T(8,128)(2,1)S(1)}, u32[]{:S(2)}, u32[]{:S(2)}) collective-permute-start(bf16[1024,256]{1,0:T(8,128)(2,1)S(1)} %collective-permute-done.4), channel_id=1, source_target_pairs={{0,16},{1,17},{2,18},{3,19},{4,20},{5,21},{6,22},{7,23},{8,24},{9,... | collective-permute-start | bytes 1572872 | tf_op jit(solution)/shard_map/ppermute | solution.py:17
  501.8 12.6 %collective-permute-start.6 = (bf16[1024,256]{1,0:T(8,128)(2,1)S(1)}, bf16[1024,256]{1,0:T(8,128)(2,1)}, u32[]{:S(2)}, u32[]{:S(2)}) collective-permute-start(bf16[1024,256]{1,0:T(8,128)(2,1)S(1)} %dynamic-slice_bitcast_fusion.2), channel_id=1, source_target_pairs={{0,16},{1,17},{2,18},{3,19},{4,20},{5,21},{6,22},{7,23},{8,24},{9,... | collective-permute-start | bytes 1572872 | tf_op jit(solution)/shard_map/ppermute | solution.py:17
  509.5 35.2 %all-gather.13.cloned.1.call-start = ((), (), s32[]{:S(2)}) async-start(), calls=%async_computation.7 | async-start | bytes 1572864 | tf_op jit(solution)/shard_map/all_gather | solution.py:31
  514.4 8.4 %collective-permute-start.7 = (bf16[1024,256]{1,0:T(8,128)(2,1)}, bf16[1024,256]{1,0:T(8,128)(2,1)S(1)}, u32[]{:S(2)}, u32[]{:S(2)}) collective-permute-start(bf16[1024,256]{1,0:T(8,128)(2,1)} %collective-permute-done.6), channel_id=1, source_target_pairs={{0,16},{1,17},{2,18},{3,19},{4,20},{5,21},{6,22},{7,23},{8,24},{9,... | collective-permute-start | bytes 1572872 | tf_op jit(solution)/shard_map/ppermute | solution.py:17
  523.8 21.0 %copy-start.6 = (bf16[2048,256]{1,0:T(8,128)(2,1)S(1)}, bf16[2048,256]{1,0:T(8,128)(2,1)}, u32[]{:S(2)}) copy-start(bf16[2048,256]{1,0:T(8,128)(2,1)} %all-gather.7.cloned.1.call-done) | copy-start | bytes 3145732
  (16 other events, 69.8 us)
Sparse Core Ops, SparseCore 0:
  223.5 18.4 all-gather.6
  244.2 13.6 all-gather.8
  373.7 18.5 all-gather.14
  393.8 14.0 all-gather.16
  411.0 35.2 all-reduce.4
  509.7 19.7 all-gather.10
  531.7 13.0 all-gather.12
where the time goes:
time: 621 us; the launch traced here: 612 us
  waiting for transfers between devices  306 us (49%)
  blocking collectives  84.6 us (14%)
  matrix products  54.4 us (9%)
  starting transfers between devices  51.9 us (8%)
  local copies, waits for them, and re-layouts  51.8 us (8%)
  other arithmetic  47.1 us (8%)
  between operations  15.6 us (3%)
    ppermute x12, waiting for transfers between devices, relay(): return lax.ppermute(block, ('dp', 'expert'), route)  277 us
    all_to_all x1, blocking collectives, local(): lax.all_to_all(send_x, 'expert', split_axis=0, concat_axis=0, tiled=True)  84.6 us
    all_gather x6, waiting for transfers between devices, migrate(): return tuple((lax.all_gather(m, 'dp', axis=0, tiled=True) for m in moved))  29.1 us
    ppermute x12, starting transfers between devices, relay(): return lax.ppermute(block, ('dp', 'expert'), route)  18.9 us
    all_to_all x1, starting transfers between devices, local(): lax.all_to_all(part.reshape(nexp, slots, width), 'expert', split_axis=0,...  15.6 us
  transfers between devices with their start and end apart: 22, of which 15 were waited for; matrix products, arithmetic and copies ran while one was open for 10% of the time, Pallas kernels for 0%

commit v1 on v0

--- a/solution.py
+++ b/solution.py
@@ -2,6 +2,7 @@
 import jax.numpy as jnp
 from jax import lax
 from jax.sharding import PartitionSpec as P
+from jax.lax import all_to_all, psum
 
 GROUP = 4
 
@@ -28,7 +29,14 @@
         )
     )
     moved = relay(relay(halves, step), step)
-    return tuple((lax.all_gather(m, "dp", axis=0, tiled=True) for m in moved))
+    return tuple(
+        (
+            jnp.concatenate(
+                all_to_all(jnp.stack([m for _ in range(psum(1, "dp"))], axis=0), "dp", 0, 0), axis=0
+            )
+            for m in moved
+        )
+    )
 
 
 def gelu_tanh(value):

time: 621 us -> 584 us (0.940)
  the two profiles are of different devices: /device:TPU:1 before, /device:TPU:76 now
where the time goes in v1:
time: 584 us; the launch traced here: 574 us
  waiting for transfers between devices  245 us (42%)
  blocking collectives  98.2 us (17%)
  starting transfers between devices  67.1 us (11%)
  local copies, waits for them, and re-layouts  51.2 us (9%)
  other arithmetic  50 us (9%)
  matrix products  46.8 us (8%)
  between operations  15.6 us (3%)
    all_to_all x1, blocking collectives, local(): lax.all_to_all(send_x, 'expert', split_axis=0, concat_axis=0, tiled=True)  81.7 us
    all_to_all x1, waiting for transfers between devices, local(): lax.all_to_all(part.reshape(nexp, slots, width), 'expert', split_axis=0,...  75.2 us
    all_to_all x1, waiting for transfers between devices, local(): lax.all_to_all(send_g, 'expert', split_axis=0, concat_axis=0, tiled=True)  73.6 us
    all_to_all x1, waiting for transfers between devices, local(): lax.all_to_all(xpart.reshape(nexp, slots, width), 'expert', split_axis=0,...  70 us
    ppermute x12, waiting for transfers between devices, relay(): return lax.ppermute(block, ('dp', 'expert'), route)  24.3 us
    ppermute x12, starting transfers between devices, relay(): return lax.ppermute(block, ('dp', 'expert'), route)  17.6 us
    all_to_all x3, blocking collectives, migrate(): all_to_all(jnp.stack([m for _ in range(psum(1, 'dp'))], axis=0), 'dp', 0, 0)  16.5 us
    all_to_all x1, starting transfers between devices, local(): lax.all_to_all(xpart.reshape(nexp, slots, width), 'expert', split_axis=0,...  14.3 us
  transfers between devices with their start and end apart: 19, of which 12 were waited for; matrix products, arithmetic and copies ran while one was open for 15% of the time, Pallas kernels for 0%

profile of v1, /device:TPU:76, one launch (start us, length us, event | category | flops | bytes accessed | tf_op | source)
XLA Modules:
  0.0 574.1 jit_solution(18038934507606744217)
XLA Ops:
  42.3 10.6 %broadcast_select_fusion = (bf16[64,24,2048]{2,1,0:T(8,128)(2,1)}, bf16[64,24,2048]{2,1,0:T(8,128)(2,1)}) fusion(bf16[64,24,2048]{2,1,0:T(8,128)(2,1)} %gather_fusion.3, pred[64]{0:T(512)(128)(4,1)S(1)} %get-tuple-element.31, bf16[64,24,2048]{2,1,0:T(8,128)(2,1)} %gather_fusion.1), kind=kLoop, calls=%fused_computation.13 | loop fusion | flops 6291456 | bytes 25165888 | tf_op jit(solution)/shard_map/jit(_take)/select_n | solution.py:118
  59.7 4.6 all_to_all.50
  64.3 81.7 %all_to_all.51 = bf16[64,24,2048]{2,1,0:T(8,128)(2,1)} all-to-all(bf16[64,24,2048]{2,1,0:T(8,128)(2,1)} %get-tuple-element.40), channel_id=1, replica_groups=mesh['dp'=2,'expert'=64] {'expert'}, dimensions={0} | all-to-all | bytes 12582912 | tf_op jit(solution)/shard_map/all_to_all | solution.py:120
  145.9 9.8 %all-to-all-start.4 = ((bf16[64,24,2048]{2,1,0:T(8,128)(2,1)}), bf16[64,24,2048]{2,1,0:T(8,128)(2,1)}, u32[]{:S(2)}, u32[]{:S(2)}) async-start(bf16[64,24,2048]{2,1,0:T(8,128)(2,1)} %get-tuple-element.39), calls=%async_computation.4 | async-start | bytes 12582912 | tf_op jit(solution)/shard_map/all_to_all | solution.py:121
  163.8 73.6 %all-to-all-done.4 = bf16[64,24,2048]{2,1,0:T(8,128)(2,1)} async-done(((bf16[64,24,2048]{2,1,0:T(8,128)(2,1)}), bf16[64,24,2048]{2,1,0:T(8,128)(2,1)}, u32[]{:S(2)}, u32[]{:S(2)}) %all-to-all-start.4) | async-done | bytes 6291488 | tf_op jit(solution)/shard_map/all_to_all | solution.py:121
  237.5 6.6 %fusion.40 = f32[256,2048]{1,0:T(8,128)} fusion(bf16[1536,2048]{1,0:T(8,128)(2,1)} %bitcast.19, f32[1536,256]{1,0:T(8,128)} %fusion.41), kind=kOutput, calls=%fused_computation.106 | convolution fusion | flops 1614151680 | bytes 9961472 | tf_op jit(solution)/shard_map/dot_general | solution.py:141
  244.1 5.6 fusion.14
  256.4 4.5 collective-permute-start.6
  288.0 4.6 all-to-all-start.6
  306.1 6.6 %all_to_all.52 = bf16[2,1024,256]{2,1,0:T(8,128)(2,1)} all-to-all(bf16[2,1024,256]{2,1,0:T(8,128)(2,1)} %pad_maximum_fusion.3), channel_id=1, replica_groups=mesh['dp'=2,'expert'=64] {'dp'}, dimensions={0} | all-to-all | bytes 2097152 | tf_op jit(solution)/shard_map/all_to_all | solution.py:35
  312.7 4.4 all-to-all-start.8
  317.2 5.9 %subtract_bitcast_fusion.1 = (f32[1,2048,256]{2,1,0:T(8,128)}, bf16[2048,256]{1,0:T(8,128)(2,1)S(1)}, bf16[1,2048,256]{2,1,0:T(8,128)(2,1)}, bf16[1,2048,256]{2,1,0:T(8,128)(2,1)}) fusion(f32[2048,256]{1,0:T(8,128)} %get-tuple-element.23, bf16[1,2048,256]{2,1,0:T(8,128)(2,1)} %param.26, bf16[2,1024,256]{2,1,0:T(8,128)(2,1)} %all-to-all-done.6, pred[]{:T(512)S(6)} %ne.24, ...), kind=kLoop, calls=%fused_computation.29 | loop fusion | flops 12582912 | bytes 14680065 | tf_op jit(solution)/shard_map/broadcast_in_dim | solution.py:170
  323.1 4.5 convolution_convert_fusion
  327.6 5.4 all_to_all.53
  332.9 14.3 %all-to-all-start.5 = ((bf16[64,24,2048]{2,1,0:T(8,128)(2,1)}), bf16[64,24,2048]{2,1,0:T(8,128)(2,1)}, u32[]{:S(2)}, u32[]{:S(2)}) async-start(bf16[64,24,2048]{2,1,0:T(8,128)(2,1)} %bitcast.148), calls=%async_computation.5 | async-start | bytes 12582912 | tf_op jit(solution)/shard_map/all_to_all | solution.py:148
  347.2 5.5 subtract_bitcast_fusion
  352.7 4.5 convolution_convert_fusion.1
  357.3 70.0 %all-to-all-done.5 = bf16[64,24,2048]{2,1,0:T(8,128)(2,1)} async-done(((bf16[64,24,2048]{2,1,0:T(8,128)(2,1)}), bf16[64,24,2048]{2,1,0:T(8,128)(2,1)}, u32[]{:S(2)}, u32[]{:S(2)}) %all-to-all-start.5) | async-done | bytes 6291488 | tf_op jit(solution)/shard_map/all_to_all | solution.py:148
  427.3 12.8 %all-to-all-start.3 = ((bf16[64,24,2048]{2,1,0:T(8,128)(2,1)}), bf16[64,24,2048]{2,1,0:T(8,128)(2,1)}, u32[]{:S(2)}, u32[]{:S(2)}) async-start(bf16[64,24,2048]{2,1,0:T(8,128)(2,1)} %bitcast.149), calls=%async_computation.3 | async-start | bytes 12582912 | tf_op jit(solution)/shard_map/all_to_all | solution.py:145
  440.1 9.5 %fusion = f32[16,24,2048]{2,0,1:T(8,128)S(1)} fusion(bf16[64,24,2048]{2,1,0:T(8,128)(2,1)} %all-to-all-done.5, s32[64]{0:T(128)S(1)} %get-tuple-element.32), kind=kOutput, calls=%fused_computation.9 | convolution fusion | flops 100664320 | bytes 9437440 | tf_op jit(solution)/shard_map/je,jcd->ecd/dot_general | solution.py:159
  451.4 75.2 %all-to-all-done.3 = bf16[64,24,2048]{2,1,0:T(8,128)(2,1)} async-done(((bf16[64,24,2048]{2,1,0:T(8,128)(2,1)}), bf16[64,24,2048]{2,1,0:T(8,128)(2,1)}, u32[]{:S(2)}, u32[]{:S(2)}) %all-to-all-start.3) | async-done | bytes 6291488 | tf_op jit(solution)/shard_map/all_to_all | solution.py:145
  526.6 9.7 %fusion.2 = f32[16,24,2048]{2,0,1:T(8,128)S(1)} fusion(bf16[64,24,2048]{2,1,0:T(8,128)(2,1)} %all-to-all-done.3, s32[64]{0:T(128)S(1)} %get-tuple-element.32), kind=kOutput, calls=%fused_computation.11 | convolution fusion | flops 100664320 | bytes 9437440 | tf_op jit(solution)/shard_map/je,jcd->ecd/dot_general | solution.py:158
  540.4 5.5 gather_fusion.4
  548.6 5.0 broadcast_select_fusion.2
  (139 shorter events, 118.1 us)
Async XLA Ops:
  7.2 25.4 %copy-start = (s32[64]{0:T(128)S(1)}, s32[64]{0:T(128)}, u32[]{:S(2)}) copy-start(s32[64]{0:T(128)} %param.22) | copy-start | bytes 772
  9.3 31.2 %collective-permute-start = (bf16[1024,256]{1,0:T(8,128)(2,1)}, bf16[1024,256]{1,0:T(8,128)(2,1)}, u32[]{:S(2)}, u32[]{:S(2)}) collective-permute-start(bf16[1024,256]{1,0:T(8,128)(2,1)} %dynamic-slice_convert_fusion.1), channel_id=1, source_target_pairs={{0,16},{1,17},{2,18},{3,19},{4,20},{5,21},{6,22},{7,23},{8,24},{9,... | collective-permute-start | bytes 1572872 | tf_op jit(solution)/shard_map/ppermute | solution.py:18
  13.0 27.7 %collective-permute-start.2 = (bf16[128,2048]{1,0:T(8,128)(2,1)}, bf16[128,2048]{1,0:T(8,128)(2,1)}, u32[]{:S(2)}, u32[]{:S(2)}) collective-permute-start(bf16[128,2048]{1,0:T(8,128)(2,1)} %dynamic-slice_convert_fusion), channel_id=1, source_target_pairs={{0,16},{1,17},{2,18},{3,19},{4,20},{5,21},{6,22},{7,23},{8,24},{9,... | collective-permute-start | bytes 1572872 | tf_op jit(solution)/shard_map/ppermute | solution.py:18
  40.5 12.4 %collective-permute-start.1 = (bf16[1024,256]{1,0:T(8,128)(2,1)}, bf16[1024,256]{1,0:T(8,128)(2,1)S(1)}, u32[]{:S(2)}, u32[]{:S(2)}) collective-permute-start(bf16[1024,256]{1,0:T(8,128)(2,1)} %collective-permute-done), channel_id=1, source_target_pairs={{0,16},{1,17},{2,18},{3,19},{4,20},{5,21},{6,22},{7,23},{8,24},{9,... | collective-permute-start | bytes 1572872 | tf_op jit(solution)/shard_map/ppermute | solution.py:18
  40.7 16.8 %collective-permute-start.3 = (bf16[128,2048]{1,0:T(8,128)(2,1)}, bf16[128,2048]{1,0:T(8,128)(2,1)S(1)}, u32[]{:S(2)}, u32[]{:S(2)}) collective-permute-start(bf16[128,2048]{1,0:T(8,128)(2,1)} %collective-permute-done.2), channel_id=1, source_target_pairs={{0,16},{1,17},{2,18},{3,19},{4,20},{5,21},{6,22},{7,23},{8,24},{9,... | collective-permute-start | bytes 1572872 | tf_op jit(solution)/shard_map/ppermute | solution.py:18
  54.0 5.7 all-to-all-start.1
  59.7 86.2 %copy-start.6 = (bf16[2,1024,256]{2,1,0:T(8,128)(2,1)}, bf16[2,1024,256]{2,1,0:T(8,128)(2,1)S(1)}, u32[]{:S(2)}) copy-start(bf16[2,1024,256]{2,1,0:T(8,128)(2,1)S(1)} %all-to-all-done.1) | copy-start | bytes 3145732
  145.9 11.1 %copy-start.3 = (f32[1,2048,256]{2,1,0:T(8,128)S(1)}, f32[1,2048,256]{2,1,0:T(8,128)}, u32[]{:S(2)}) copy-start(f32[1,2048,256]{2,1,0:T(8,128)} %param.24) | copy-start | bytes 6291460
  145.9 91.5 %all-to-all-start.4 = ((bf16[64,24,2048]{2,1,0:T(8,128)(2,1)}), bf16[64,24,2048]{2,1,0:T(8,128)(2,1)}, u32[]{:S(2)}, u32[]{:S(2)}) async-start(bf16[64,24,2048]{2,1,0:T(8,128)(2,1)} %get-tuple-element.39), calls=%async_computation.4 | async-start | bytes 12582912 | tf_op jit(solution)/shard_map/all_to_all | solution.py:121
  155.7 161.5 %all-reduce.5.cloned.1.call-start = ((), (), s32[]{:S(2)}) async-start(), calls=%async_computation.10 | async-start | bytes 8388608 | tf_op jit(solution)/shard_map/psum | solution.py:152
  237.5 13.2 %slice-start.1 = ((s8[6291456]{0:T(1024)(128)(4,1)}), s8[4194304]{0:T(1024)(128)(4,1)S(1)}, s32[]{:S(2)}) async-start(s8[6291456]{0:T(1024)(128)(4,1)} %bitcast.157), calls=%async_computation.12 | async-start | bytes 8388608
  255.2 9.3 %collective-permute-start.4 = (bf16[1024,256]{1,0:T(8,128)(2,1)S(1)}, bf16[1024,256]{1,0:T(8,128)(2,1)S(1)}, u32[]{:S(2)}, u32[]{:S(2)}) collective-permute-start(bf16[1024,256]{1,0:T(8,128)(2,1)S(1)} %dynamic-slice_bitcast_fusion.3), channel_id=1, source_target_pairs={{0,16},{1,17},{2,18},{3,19},{4,20},{5,21},{6,22},{7,23},{8,24},{9,... | collective-permute-start | bytes 1572872 | tf_op jit(solution)/shard_map/ppermute | solution.py:18
  256.4 13.8 %collective-permute-start.6 = (bf16[1024,256]{1,0:T(8,128)(2,1)S(1)}, bf16[1024,256]{1,0:T(8,128)(2,1)}, u32[]{:S(2)}, u32[]{:S(2)}) collective-permute-start(bf16[1024,256]{1,0:T(8,128)(2,1)S(1)} %dynamic-slice_bitcast_fusion.2), channel_id=1, source_target_pairs={{0,16},{1,17},{2,18},{3,19},{4,20},{5,21},{6,22},{7,23},{8,24},{9,... | collective-permute-start | bytes 1572872 | tf_op jit(solution)/shard_map/ppermute | solution.py:18
  261.0 14.8 %collective-permute-start.8 = (bf16[128,2048]{1,0:T(8,128)(2,1)S(1)}, bf16[128,2048]{1,0:T(8,128)(2,1)}, u32[]{:S(2)}, u32[]{:S(2)}) collective-permute-start(bf16[128,2048]{1,0:T(8,128)(2,1)S(1)} %dynamic-slice_bitcast_fusion.1), channel_id=1, source_target_pairs={{0,16},{1,17},{2,18},{3,19},{4,20},{5,21},{6,22},{7,23},{8,24},{9,... | collective-permute-start | bytes 1572872 | tf_op jit(solution)/shard_map/ppermute | solution.py:18
  261.1 20.3 %collective-permute-start.10 = (bf16[128,2048]{1,0:T(8,128)(2,1)S(1)}, bf16[128,2048]{1,0:T(8,128)(2,1)}, u32[]{:S(2)}, u32[]{:S(2)}) collective-permute-start(bf16[128,2048]{1,0:T(8,128)(2,1)S(1)} %dynamic-slice_bitcast_fusion), channel_id=1, source_target_pairs={{0,16},{1,17},{2,18},{3,19},{4,20},{5,21},{6,22},{7,23},{8,24},{9,... | collective-permute-start | bytes 1572872 | tf_op jit(solution)/shard_map/ppermute | solution.py:18
  264.5 22.5 %collective-permute-start.5 = (bf16[1024,256]{1,0:T(8,128)(2,1)S(1)}, bf16[1024,256]{1,0:T(8,128)(2,1)S(1)}, u32[]{:S(2)}, u32[]{:S(2)}) collective-permute-start(bf16[1024,256]{1,0:T(8,128)(2,1)S(1)} %collective-permute-done.4), channel_id=1, source_target_pairs={{0,16},{1,17},{2,18},{3,19},{4,20},{5,21},{6,22},{7,23},{8,24},{9,... | collective-permute-start | bytes 1572872 | tf_op jit(solution)/shard_map/ppermute | solution.py:18
  270.2 22.5 %collective-permute-start.7 = (bf16[1024,256]{1,0:T(8,128)(2,1)}, bf16[1024,256]{1,0:T(8,128)(2,1)}, u32[]{:S(2)}, u32[]{:S(2)}) collective-permute-start(bf16[1024,256]{1,0:T(8,128)(2,1)} %collective-permute-done.6), channel_id=1, source_target_pairs={{0,16},{1,17},{2,18},{3,19},{4,20},{5,21},{6,22},{7,23},{8,24},{9,... | collective-permute-start | bytes 1572872 | tf_op jit(solution)/shard_map/ppermute | solution.py:18
  275.8 22.5 %collective-permute-start.9 = (bf16[128,2048]{1,0:T(8,128)(2,1)}, bf16[128,2048]{1,0:T(8,128)(2,1)}, u32[]{:S(2)}, u32[]{:S(2)}) collective-permute-start(bf16[128,2048]{1,0:T(8,128)(2,1)} %collective-permute-done.8), channel_id=1, source_target_pairs={{0,16},{1,17},{2,18},{3,19},{4,20},{5,21},{6,22},{7,23},{8,24},{9,... | collective-permute-start | bytes 1572872 | tf_op jit(solution)/shard_map/ppermute | solution.py:18
  281.4 22.5 %collective-permute-start.11 = (bf16[128,2048]{1,0:T(8,128)(2,1)}, bf16[128,2048]{1,0:T(8,128)(2,1)}, u32[]{:S(2)}, u32[]{:S(2)}) collective-permute-start(bf16[128,2048]{1,0:T(8,128)(2,1)} %collective-permute-done.10), channel_id=1, source_target_pairs={{0,16},{1,17},{2,18},{3,19},{4,20},{5,21},{6,22},{7,23},{8,24},{9,... | collective-permute-start | bytes 1572872 | tf_op jit(solution)/shard_map/ppermute | solution.py:18
  288.0 18.2 %all-to-all-start.6 = ((bf16[2,1024,256]{2,1,0:T(8,128)(2,1)}), bf16[2,1024,256]{2,1,0:T(8,128)(2,1)}, u32[]{:S(2)}, u32[]{:S(2)}) async-start(bf16[2,1024,256]{2,1,0:T(8,128)(2,1)} %pad_maximum_fusion.2), calls=%async_computation.6 | async-start | bytes 2097152 | tf_op jit(solution)/shard_map/all_to_all | solution.py:35
  312.7 14.8 %all-to-all-start.8 = ((bf16[2,128,2048]{2,1,0:T(8,128)(2,1)}), bf16[2,128,2048]{2,1,0:T(8,128)(2,1)}, u32[]{:S(2)}, u32[]{:S(2)}) async-start(bf16[2,128,2048]{2,1,0:T(8,128)(2,1)} %pad_maximum_fusion.4), calls=%async_computation.8 | async-start | bytes 2097152 | tf_op jit(solution)/shard_map/all_to_all | solution.py:35
  332.9 14.3 %copy-start.5 = (f32[1,256,2048]{2,1,0:T(8,128)S(1)}, f32[1,256,2048]{2,1,0:T(8,128)}, u32[]{:S(2)}) copy-start(f32[1,256,2048]{2,1,0:T(8,128)} %param.25) | copy-start | bytes 6291460
  332.9 94.4 %all-to-all-start.5 = ((bf16[64,24,2048]{2,1,0:T(8,128)(2,1)}), bf16[64,24,2048]{2,1,0:T(8,128)(2,1)}, u32[]{:S(2)}, u32[]{:S(2)}) async-start(bf16[64,24,2048]{2,1,0:T(8,128)(2,1)} %bitcast.148), calls=%async_computation.5 | async-start | bytes 12582912 | tf_op jit(solution)/shard_map/all_to_all | solution.py:148
  427.3 99.3 %all-to-all-start.3 = ((bf16[64,24,2048]{2,1,0:T(8,128)(2,1)}), bf16[64,24,2048]{2,1,0:T(8,128)(2,1)}, u32[]{:S(2)}, u32[]{:S(2)}) async-start(bf16[64,24,2048]{2,1,0:T(8,128)(2,1)} %bitcast.149), calls=%async_computation.3 | async-start | bytes 12582912 | tf_op jit(solution)/shard_map/all_to_all | solution.py:145
  (20 other events, 90.0 us)
Sparse Core Ops, SparseCore 0:
  254.1 38.9 all-reduce.4
